TPU v7x, 128 devices: a whole 4x4x4 slice. The times are simulated.
128 devices in a mesh: layer: 4 (over x_hi, core), feat: 16 (over z, y), par: 2 (over x_lo).
Axes of the slice: x: 4 (x_hi: 2, x_lo: 2; x = x_hi * 2 + x_lo), y: 4, z: 4, core: 2. Of those that a mesh axis runs over, the one named last changes fastest.
Arguments:
- residual: bfloat16 [4, 512, 2304], P('layer'), may hold values from -6 to 6
- norm_gain: float32 [4, 2304], P('layer'), may hold values from 0.5 to 1.5
- gate_weight: bfloat16 [4, 2304, 9216], P('layer', None, ('feat', 'par')), may hold values from -0.125 to 0.125
- up_weight: bfloat16 [4, 2304, 9216], P('layer', None, ('feat', 'par')), may hold values from -0.125 to 0.125
- down_weight: bfloat16 [4, 9216, 2304], P('layer', ('feat', 'par')), may hold values from -0.0625 to 0.0625
- enc_weight: float32 [4, 2304, 8192], P('layer', 'par', 'feat'), may hold values from -0.125 to 0.125
- enc_bias: float32 [4, 8192], P('layer', 'feat'), may hold values from -1 to 0.5
- dec_weight: bfloat16 [4, 2, 2, 8192, 2304], P('layer', 'par', None, 'feat'), may hold values from -0.0625 to 0.0625
- dec_bias: float32 [4, 2304], replicated, may hold values from -3 to 3
Outputs:
- enc_grad: float32 [4, 2304, 8192], P('layer', 'par', 'feat')
- enc_bias_grad: float32 [4, 8192], P('layer', 'feat')
- dec_grad: bfloat16 [4, 2, 2, 8192, 2304], P('layer', 'par', None, 'feat')
All inputs are finite; a program needn't handle non-finite values.
Results may differ from a plain program's by a relative error of at most 0.007.
Values may be sent and summed in bfloat16 or wider, within the bound.
A program may use at most 192 MiB of HBM per device.

v0:
```python
import jax
import jax.numpy as jnp
from jax import lax
from jax.sharding import PartitionSpec as P


def rms_normed(rows_in, gain_row):
    values = rows_in.astype(jnp.float32)
    scaling = lax.rsqrt(jnp.mean(values * values, axis=-1, keepdims=True) + 1e-06)
    return (values * scaling * gain_row).astype(jnp.bfloat16)


def shards(
    residual,
    norm_gain,
    gate_weight,
    up_weight,
    down_weight,
    enc_weight,
    enc_bias,
    dec_weight,
    dec_bias,
):
    highest = lax.Precision.HIGHEST
    source = lax.axis_index("layer")
    parity = lax.axis_index("par")
    slot_count = dec_weight.shape[2]
    normed = rms_normed(residual[0], norm_gain[0])
    tokens, model_width = normed.shape
    gate_value = jnp.dot(normed, gate_weight[0], preferred_element_type=jnp.float32)
    up_value = jnp.dot(normed, up_weight[0], preferred_element_type=jnp.float32)
    hidden = (jax.nn.gelu(gate_value, approximate=True) * up_value).astype(jnp.bfloat16)
    target_part = jnp.dot(hidden, down_weight[0], preferred_element_type=jnp.float32)
    half_width = enc_weight.shape[1]
    my_rows = lax.dynamic_slice_in_dim(normed, parity * half_width, half_width, 1).astype(
        jnp.float32
    )
    pre_part = jnp.dot(my_rows, enc_weight[0], precision=highest)
    pre_act = lax.psum(pre_part, "par") + enc_bias[0]
    positive = jnp.maximum(pre_act, 0.0)
    actives = (positive * positive).astype(jnp.bfloat16)
    slot_ids = jnp.arange(slot_count, dtype=jnp.int32)
    slot_live = 2 * slot_ids + parity >= source
    live_float = slot_live.astype(jnp.float32)
    decoders = dec_weight[0, 0]
    recon_parts = (
        jnp.einsum("tf,jfd->jtd", actives, decoders, preferred_element_type=jnp.float32)
        * live_float[:, None, None]
    )
    bias_slots = lax.dynamic_index_in_dim(
        dec_bias.reshape(slot_count, 2, model_width), parity, 1, keepdims=False
    )
    full_target = lax.psum(target_part, ("feat", "par"))
    all_targets = lax.all_gather(full_target[None], "layer", axis=0, tiled=True)
    target_slots = lax.dynamic_index_in_dim(
        all_targets.reshape(slot_count, 2, tokens, model_width), parity, 1, keepdims=False
    )
    summed_rows = lax.psum(recon_parts, ("layer", "feat"))
    err_full = summed_rows + bias_slots[:, None, :]
    err_full = err_full - target_slots
    errors = (err_full * 0.0625).astype(jnp.bfloat16)
    masked = errors * slot_live.astype(jnp.bfloat16)[:, None, None]
    back_part = jnp.einsum("jtd,jfd->tf", masked, decoders, preferred_element_type=jnp.float32)
    back_grad = lax.psum(back_part.astype(jnp.bfloat16), "par").astype(jnp.float32)
    d_pre = back_grad * 2.0 * positive
    enc_grad = lax.dot_general(my_rows, d_pre, (((0,), (0,)), ((), ())), precision=highest)
    bias_grad = jnp.sum(d_pre, axis=0)
    dec_grad = jnp.einsum(
        "tf,jtd->jfd", actives, masked, preferred_element_type=jnp.float32
    ).astype(jnp.bfloat16)
    return (enc_grad[None], bias_grad[None], dec_grad[None, None])


def solution(mesh):
    return jax.shard_map(
        shards,
        mesh=mesh,
        in_specs=(
            P("layer", None, None),
            P("layer", None),
            P("layer", None, ("feat", "par")),
            P("layer", None, ("feat", "par")),
            P("layer", ("feat", "par"), None),
            P("layer", "par", "feat"),
            P("layer", "feat"),
            P("layer", "par", None, "feat", None),
            P(),
        ),
        out_specs=(
            P("layer", "par", "feat"),
            P("layer", "feat"),
            P("layer", "par", None, "feat", None),
        ),
        check_vma=False,
    )
```

profile of v0, /device:TPU:1, one launch (start us, length us, event | category | flops | bytes accessed | tf_op | source)
XLA Modules:
  0.0 1276.6 jit_solution(10719600831375024537)
XLA Ops:
  7.2 0.0 copy-start
  7.2 0.0 all-reduce.5.cloned.1.call-start
  7.2 2.4 multiply_reduce_fusion
  9.6 4.2 convert_bitcast_fusion
  13.8 0.1 dynamic-slice
  13.9 4.9 fusion.12
  18.8 0.0 all-reduce.5.cloned.1.call-update
  18.9 0.0 copy-start.2
  18.9 0.0 all-reduce.9.cloned.1.call-start
  18.9 3.2 fusion.43
  22.2 6.3 convolution_bitcast_fusion
  28.4 0.0 all-reduce.9.cloned.1.call-update
  28.5 0.0 all-reduce.7.cloned.1.call-start
  28.5 40.3 %all-reduce.5.cloned.1.call-done = f32[512,512]{1,0:T(8,128)} async-done(((f32[512,512]{1,0:T(8,128)}), f32[512,512]{1,0:T(8,128)}) %all-reduce.5.cloned.1.call-update) | async-done | bytes 1048592 | tf_op jit(solution)/shard_map/psum | solution.py:39
  68.8 0.0 copy-done.5
  68.8 8.9 multiply_bitcast_fusion
  77.8 0.0 all-reduce.7.cloned.1.call-update
  77.8 0.0 copy-start.4
  77.8 0.0 all-gather.2.cloned.1.call-start
  77.8 314.6 %all-reduce.9.cloned.1.call-done = f32[1,512,2304]{2,1,0:T(8,128)} async-done(((f32[1,512,2304]{2,1,0:T(8,128)}), f32[1,512,2304]{2,1,0:T(8,128)}) %all-reduce.9.cloned.1.call-update) | async-done | bytes 4718608 | tf_op jit(solution)/shard_map/psum | solution.py:53
  392.4 0.0 all-gather.2.cloned.1.call-update
  392.5 0.2 all-reduce.11.cloned.1.call-start
  392.8 668.2 %all-reduce.7.cloned.1.call-done = f32[2,512,2304]{2,1,0:T(8,128)} async-done(((f32[2,512,2304]{2,1,0:T(8,128)}), f32[2,512,2304]{2,1,0:T(8,128)}) %all-reduce.7.cloned.1.call-update) | async-done | bytes 9437200 | tf_op jit(solution)/shard_map/psum | solution.py:58
  1061.0 149.9 %all-gather.2.cloned.1.call-done = f32[4,512,2304]{2,1,0:T(8,128)} async-done(((f32[1,512,2304]{2,1,0:T(8,128)}), f32[4,512,2304]{2,1,0:T(8,128)}) %all-gather.2.cloned.1.call-update) | async-done | bytes 18874384 | tf_op jit(solution)/shard_map/all_gather | solution.py:54
  1210.8 10.1 fusion.5
  1220.9 7.3 fusion.22
  1228.2 0.0 all-reduce.11.cloned.1.call-update
  1228.2 6.7 fusion.2
  1234.9 6.8 copy.17
  1241.7 21.0 %all-reduce.11.cloned.1.call-done = bf16[512,512]{1,0:T(8,128)(2,1)} async-done(((bf16[512,512]{1,0:T(8,128)(2,1)}), bf16[512,512]{1,0:T(8,128)(2,1)}) %all-reduce.11.cloned.1.call-update) | async-done | bytes 524304 | tf_op jit(solution)/shard_map/psum | solution.py:64
  1262.7 1.8 fusion.48
  1264.6 5.5 convolution_bitcast_fusion.1
  (17 shorter events, 0.1 us)
Async XLA Ops:
  7.2 6.7 copy-start
  7.2 61.7 %all-reduce.5.cloned.1.call-start = ((), (), s32[]{:S(2)}) async-start(), calls=%async_computation | async-start | bytes 2097152 | tf_op jit(solution)/shard_map/psum | solution.py:39
  7.2 6.5 copy-start.6
  18.9 3.3 copy-start.2
  18.9 373.6 %all-reduce.9.cloned.1.call-start = ((), (), s32[]{:S(2)}) async-start(), calls=%async_computation.2 | async-start | bytes 9437184 | tf_op jit(solution)/shard_map/psum | solution.py:53
  28.4 40.4 %copy-start.5 = (f32[1,512]{1,0:T(1,128)S(1)}, f32[1,512]{1,0:T(1,128)}, u32[]{:S(2)}) copy-start(f32[1,512]{1,0:T(1,128)} %param.15) | copy-start | bytes 6148
  28.5 1032.5 %all-reduce.7.cloned.1.call-start = ((), (), s32[]{:S(2)}) async-start(), calls=%async_computation.1 | async-start | bytes 18874368 | tf_op jit(solution)/shard_map/psum | solution.py:58
  77.8 314.9 %copy-start.4 = (f32[4,2304]{1,0:T(4,128)S(1)}, f32[4,2304]{1,0:T(4,128)}, u32[]{:S(2)}) copy-start(f32[4,2304]{1,0:T(4,128)} %param.17) | copy-start | bytes 110596
  77.8 1133.0 %all-gather.2.cloned.1.call-start = ((), (), s32[]{:S(2)}) async-start(), calls=%async_computation.3 | async-start | bytes 23592960 | tf_op jit(solution)/shard_map/all_gather | solution.py:54
  392.5 870.3 %all-reduce.11.cloned.1.call-start = ((), (), s32[]{:S(2)}) async-start(), calls=%async_computation.4 | async-start | bytes 1048576 | tf_op jit(solution)/shard_map/psum | solution.py:64
  1220.9 7.3 copy-start.3
  1234.9 35.2 %copy-start.1 = (f32[1,1152,512]{2,1,0:T(8,128)S(1)}, f32[1,1152,512]{2,1,0:T(8,128)}, u32[]{:S(2)}) copy-start(f32[1,1152,512]{2,1,0:T(8,128)} %param.14) | copy-start | bytes 7077892
Sparse Core Ops, SparseCore 0:
  19.0 49.8 all-reduce.4
  72.1 320.3 all-reduce.8
  395.1 665.8 all-reduce.6
  1062.6 148.1 all-gather.1
  1228.3 34.3 all-reduce.10
where the time goes:
time: 1280 us
  waiting for transfers between devices  1190 us (93%)
  matrix products  42.9 us (3%)
  other arithmetic  18.5 us (1%)
  between operations  13.9 us (1%)
    psum x1, waiting for transfers between devices, shards(): summed_rows = lax.psum(recon_parts, ('layer', 'feat'))  668 us
    psum x1, waiting for transfers between devices, shards(): full_target = lax.psum(target_part, ('feat', 'par'))  315 us
    all_gather x1, waiting for transfers between devices, shards(): all_targets = lax.all_gather(full_target[None], 'layer', axis=0, tiled=True)  150 us
    psum x1, waiting for transfers between devices, shards(): pre_act = lax.psum(pre_part, 'par') + enc_bias[0]  40.3 us
  transfers between devices with their start and end apart: 5, of which 5 were waited for; matrix products, arithmetic and copies ran while one was open for 3% of the time, Pallas kernels for 0%

commit v1 on v0

--- a/solution.py
+++ b/solution.py
@@ -50,7 +50,7 @@
     bias_slots = lax.dynamic_index_in_dim(
         dec_bias.reshape(slot_count, 2, model_width), parity, 1, keepdims=False
     )
-    full_target = lax.psum(target_part, ("feat", "par"))
+    full_target = lax.psum(lax.psum(target_part, "par"), "feat")
     all_targets = lax.all_gather(full_target[None], "layer", axis=0, tiled=True)
     target_slots = lax.dynamic_index_in_dim(
         all_targets.reshape(slot_count, 2, tokens, model_width), parity, 1, keepdims=False

time: 1280 us -> 1160 us (0.906)
  waiting for transfers between devices: 1190 us -> 1080 us
    psum x2, waiting for transfers between devices: 355 us -> 257 us  [shards(): full_target = lax.psum(lax.psum(target_part, 'par'), 'feat')]
    psum x1, waiting for transfers between devices: 668 us -> 648 us  [shards(): summed_rows = lax.psum(recon_parts, ('layer', 'feat'))]
  transfers between devices with their start and end apart: 5 -> 5, of which waited for: 5 -> 5; matrix products, arithmetic and copies ran while one was open for 3% -> 2% of each run, Pallas kernels for 0% -> 0%
where the time goes in v1:
time: 1160 us
  waiting for transfers between devices  1080 us (93%)
  matrix products  40.4 us (3%)
  other arithmetic  18.5 us (2%)
  between operations  13.9 us (1%)
    psum x1, waiting for transfers between devices, shards(): summed_rows = lax.psum(recon_parts, ('layer', 'feat'))  648 us
    psum x2, waiting for transfers between devices, shards(): full_target = lax.psum(lax.psum(target_part, 'par'), 'feat')  257 us
    all_gather x1, waiting for transfers between devices, shards(): all_targets = lax.all_gather(full_target[None], 'layer', axis=0, tiled=True)  150 us
  transfers between devices with their start and end apart: 5, of which 5 were waited for; matrix products, arithmetic and copies ran while one was open for 2% of the time, Pallas kernels for 0%

profile of v1, /device:TPU:1, one launch (start us, length us, event | category | flops | bytes accessed | tf_op | source)
XLA Modules:
  0.0 1156.4 jit_solution(8377540999475604657)
XLA Ops:
  7.2 0.0 copy-start
  7.2 0.0 all-reduce.12.cloned.1.call-start
  7.2 2.4 multiply_reduce_fusion
  9.6 4.2 convert_bitcast_fusion
  13.8 0.1 dynamic-slice
  13.9 3.2 fusion.43
  17.1 0.2 copy-done.2
  17.3 3.3 fusion.12
  20.6 7.0 fusion.17
  27.6 0.0 all-reduce.12.cloned.1.call-update
  27.6 0.0 all-reduce.8.cloned.1.call-start
  27.7 152.1 %all-reduce.12.cloned.1.call-done = (f32[512,2304]{1,0:T(8,128)}, f32[512,512]{1,0:T(8,128)}) async-done(((f32[512,2304]{1,0:T(8,128)}, f32[512,512]{1,0:T(8,128)}), (f32[512,2304]{1,0:T(8,128)}, f32[512,512]{1,0:T(8,128)})) %all-reduce.12.cloned.1.call-update) | async-done | bytes 5767184 | tf_op jit(solution)/shard_map/psum | solution.py:53
  179.8 0.0 all-reduce.8.cloned.1.call-update
  179.8 0.0 all-reduce.6.cloned.1.call-start
  179.9 1.1 copy-done.3
  181.0 7.4 multiply_bitcast_fusion
  188.4 0.0 all-reduce.6.cloned.1.call-update
  188.4 0.0 copy-start.4
  188.4 0.0 all-gather.2.cloned.1.call-start
  188.5 104.4 %all-reduce.8.cloned.1.call-done = f32[1,512,2304]{2,1,0:T(8,128)} async-done(((f32[1,512,2304]{2,1,0:T(8,128)}), f32[1,512,2304]{2,1,0:T(8,128)}) %all-reduce.8.cloned.1.call-update) | async-done | bytes 4718608 | tf_op jit(solution)/shard_map/psum | solution.py:53
  292.9 0.0 all-gather.2.cloned.1.call-update
  292.9 0.2 all-reduce.10.cloned.1.call-start
  293.3 647.9 %all-reduce.6.cloned.1.call-done = f32[2,512,2304]{2,1,0:T(8,128)} async-done(((f32[2,512,2304]{2,1,0:T(8,128)}), f32[2,512,2304]{2,1,0:T(8,128)}) %all-reduce.6.cloned.1.call-update) | async-done | bytes 9437200 | tf_op jit(solution)/shard_map/psum | solution.py:58
  941.2 149.5 %all-gather.2.cloned.1.call-done = f32[4,512,2304]{2,1,0:T(8,128)} async-done(((f32[1,512,2304]{2,1,0:T(8,128)}), f32[4,512,2304]{2,1,0:T(8,128)}) %all-gather.2.cloned.1.call-update) | async-done | bytes 18874384 | tf_op jit(solution)/shard_map/all_gather | solution.py:54
  1090.7 10.1 fusion.5
  1100.8 7.2 fusion.23
  1107.9 0.0 all-reduce.10.cloned.1.call-update
  1108.0 6.7 fusion.2
  1114.7 6.8 copy.17
  1121.5 21.0 %all-reduce.10.cloned.1.call-done = bf16[512,512]{1,0:T(8,128)(2,1)} async-done(((bf16[512,512]{1,0:T(8,128)(2,1)}), bf16[512,512]{1,0:T(8,128)(2,1)}) %all-reduce.10.cloned.1.call-update) | async-done | bytes 524304 | tf_op jit(solution)/shard_map/psum | solution.py:64
  1142.5 1.8 fusion.48
  1144.3 5.5 convolution_bitcast_fusion
  (17 shorter events, 0.1 us)
Async XLA Ops:
  7.2 10.0 copy-start
  7.2 172.6 %all-reduce.12.cloned.1.call-start = ((), (), s32[]{:S(2)}) async-start(), calls=%async_computation.4 | async-start | bytes 11534336 | tf_op jit(solution)/shard_map/psum | solution.py:53
  7.2 6.5 copy-start.6
  13.9 3.4 copy-start.2
  27.6 152.3 %copy-start.5 = (f32[1,512]{1,0:T(1,128)S(1)}, f32[1,512]{1,0:T(1,128)}, u32[]{:S(2)}) copy-start(f32[1,512]{1,0:T(1,128)} %param.15) | copy-start | bytes 6148
  27.6 265.3 %all-reduce.8.cloned.1.call-start = ((), (), s32[]{:S(2)}) async-start(), calls=%async_computation.1 | async-start | bytes 9437184 | tf_op jit(solution)/shard_map/psum | solution.py:53
  179.8 1.2 copy-start.3
  179.8 761.3 %all-reduce.6.cloned.1.call-start = ((), (), s32[]{:S(2)}) async-start(), calls=%async_computation | async-start | bytes 18874368 | tf_op jit(solution)/shard_map/psum | solution.py:58
  188.4 104.7 %copy-start.4 = (f32[4,2304]{1,0:T(4,128)S(1)}, f32[4,2304]{1,0:T(4,128)}, u32[]{:S(2)}) copy-start(f32[4,2304]{1,0:T(4,128)} %param.17) | copy-start | bytes 110596
  188.4 902.3 %all-gather.2.cloned.1.call-start = ((), (), s32[]{:S(2)}) async-start(), calls=%async_computation.2 | async-start | bytes 23592960 | tf_op jit(solution)/shard_map/all_gather | solution.py:54
  292.9 849.6 %all-reduce.10.cloned.1.call-start = ((), (), s32[]{:S(2)}) async-start(), calls=%async_computation.3 | async-start | bytes 1048576 | tf_op jit(solution)/shard_map/psum | solution.py:64
  1114.7 35.2 %copy-start.1 = (f32[1,1152,512]{2,1,0:T(8,128)S(1)}, f32[1,1152,512]{2,1,0:T(8,128)}, u32[]{:S(2)}) copy-start(f32[1,1152,512]{2,1,0:T(8,128)} %param.14) | copy-start | bytes 7077892
Sparse Core Ops, SparseCore 0:
  27.8 151.9 all-reduce.11
  183.6 109.2 all-reduce.7
  295.4 645.7 all-reduce.5
  942.7 147.9 all-gather.1
  1108.1 34.3 all-reduce.9
